TPU v7x, 1024 devices: a whole 4x8x16 slice. The times are simulated.
1024 devices in a mesh: src: 8 (over x, y_hi), space: 128 (over z, y_lo, core).
Axes of the slice: x: 4, y: 8 (y_hi: 2, y_lo: 4; y = y_hi * 4 + y_lo), z: 16, core: 2. Of those that a mesh axis runs over, the one named last changes fastest.
Arguments:
- vectors: bfloat16 [3, 2, 147456, 128], P(None, None, 'space', 'src'), may hold values from -0.015625 to 0.015625
- lambdas: float32 [3, 128], replicated, may hold values from 0.01 to 0.2
- sources: bfloat16 [2, 147456, 1024], P(None, 'space', 'src'), may hold values from -6 to 6
Outputs:
- propagated: bfloat16 [2, 147456, 1024], P(None, 'space', 'src')
All inputs are finite; a program needn't handle non-finite values.
Results may differ from a plain program's by a relative error of at most 0.0049.
Values may be sent and summed in bfloat16 or wider, within the bound.
A program may use at most 32 MiB of HBM per device.

v0:
```python
import jax
import jax.numpy as jnp
from jax import lax
from jax.sharding import PartitionSpec as P


def project(vec_re, vec_im, src_re, src_im):
    coef_re = jnp.einsum(
        "rm,rc->mc", vec_re, src_re, preferred_element_type=jnp.float32
    ) + jnp.einsum("rm,rc->mc", vec_im, src_im, preferred_element_type=jnp.float32)
    coef_im = jnp.einsum(
        "rm,rc->mc", vec_re, src_im, preferred_element_type=jnp.float32
    ) - jnp.einsum("rm,rc->mc", vec_im, src_re, preferred_element_type=jnp.float32)
    return (coef_re, coef_im)


def scaled_coeffs(pair, lambda_rows):
    inverse = 1.0 / lambda_rows
    summed = lax.psum(pair, "space")
    scaled = (summed * inverse[None, :, :, None]).astype(jnp.bfloat16)
    return scaled


def expand(vec_re, vec_im, scaled_re, scaled_im, out_re, out_im):
    out_re = (
        out_re
        + jnp.dot(vec_re, scaled_re, preferred_element_type=jnp.float32)
        - jnp.dot(vec_im, scaled_im, preferred_element_type=jnp.float32)
    )
    out_im = (
        out_im
        + jnp.dot(vec_re, scaled_im, preferred_element_type=jnp.float32)
        + jnp.dot(vec_im, scaled_re, preferred_element_type=jnp.float32)
    )
    return (out_re, out_im)


def on_device(vectors, lambdas, sources):
    src_re = sources[0]
    src_im = sources[1]
    blocks = vectors.shape[0]
    out_re = jnp.zeros(src_re.shape, jnp.float32)
    out_im = jnp.zeros(src_re.shape, jnp.float32)
    for number in range(blocks):
        whole_block = lax.all_gather(vectors[number], "src", axis=2, tiled=True)
        partial_re, partial_im = project(whole_block[0], whole_block[1], src_re, src_im)
        pair = jnp.stack([partial_re, partial_im])[:, None]
        scaled = scaled_coeffs(pair, lambdas[number][None, :])
        out_re, out_im = expand(
            whole_block[0], whole_block[1], scaled[0, 0], scaled[1, 0], out_re, out_im
        )
    return jnp.stack([out_re, out_im]).astype(jnp.bfloat16)


def solution(mesh):
    placed = (P(None, None, "space", "src"), P(), P(None, "space", "src"))
    return jax.shard_map(
        on_device, mesh=mesh, in_specs=placed, out_specs=P(None, "space", "src"), check_vma=False
    )
```

profile of v0, /device:TPU:1, one launch (start us, length us, event | category | flops | bytes accessed | tf_op | source)
XLA Modules:
  0.0 1159.8 jit_solution(9120746454510167380)
XLA Ops:
  6.5 1.0 fusion.42
  7.6 43.9 %all-gather.2 = bf16[1,2,1152,128]{2,3,1,0:T(8,128)(2,1)S(1)} all-gather(bf16[1,2,1152,16]{2,3,1,0:T(8,128)(2,1)S(1)} %get-tuple-element.8), channel_id=4, replica_groups=mesh['src'=8,'space'=128] {'src'}, dimensions={3}, use_global_device_ids=true | all-gather | bytes 663552 | tf_op jit(solution)/shard_map/all_gather | solution.py:45
  51.9 43.3 %all-gather = bf16[1,2,1152,128]{2,3,1,0:T(8,128)(2,1)S(1)} all-gather(bf16[1,2,1152,16]{2,3,1,0:T(8,128)(2,1)S(1)} %get-tuple-element.9), channel_id=2, replica_groups=mesh['src'=8,'space'=128] {'src'}, dimensions={3}, use_global_device_ids=true | all-gather | bytes 663552 | tf_op jit(solution)/shard_map/all_gather | solution.py:45
  95.7 45.5 %all-gather.1 = bf16[1,2,1152,128]{2,3,1,0:T(8,128)(2,1)S(1)} all-gather(bf16[1,2,1152,16]{2,3,1,0:T(8,128)(2,1)S(1)} %get-tuple-element.10), channel_id=3, replica_groups=mesh['src'=8,'space'=128] {'src'}, dimensions={3}, use_global_device_ids=true | all-gather | bytes 663552 | tf_op jit(solution)/shard_map/all_gather | solution.py:45
  143.1 0.7 maximum_bitcast_fusion.2
  143.7 0.7 maximum_bitcast_fusion
  144.4 0.7 maximum_bitcast_fusion.1
  145.1 0.7 copy-done.2
  145.7 1001.1 %all-reduce.3.cloned.1.call-done = (f32[2,1,128,128]{3,2,0,1:T(8,128)}, f32[2,1,128,128]{3,2,0,1:T(8,128)}, f32[2,1,128,128]{3,2,0,1:T(8,128)}) async-done(((f32[2,1,128,128]{3,2,0,1:T(8,128)}, f32[2,1,128,128]{3,2,0,1:T(8,128)}, f32[2,1,128,128]{3,2,0,1:T(8,128)}), (f32[2,1,128,128]{3,2,0,1:T(8,128)}, f32[2,1,128,128]{3,2,0,1:T(8,128)}, f32[2,1,128,128]{3,2,0,1:T(8,128)})) %all-reduce.3.cloned.1.call-update) | async-done | bytes 393232 | tf_op jit(solution)/shard_map/psum | solution.py:19
  1146.8 1.0 multiply_convert_fusion.2
  1147.8 0.3 fusion.28
  1148.1 0.3 fusion.29
  1148.3 0.3 convolution_add_fusion.4
  1148.6 0.6 copy-done
  1149.4 0.3 convolution_add_fusion.3
  1149.7 0.3 convolution_add_fusion.2
  1149.9 0.3 convolution_add_fusion.1
  1150.2 0.3 fusion.2
  1150.5 0.3 convolution_subtract_fusion.2
  1150.7 0.3 convolution_add_fusion.6
  1151.0 0.3 convolution_subtract_fusion.1
  1151.3 0.3 convolution_add_fusion.5
  1151.5 0.3 fusion.3
  1151.9 1.1 copy.4
  (23 shorter events, 3.0 us)
Async XLA Ops:
  6.5 44.9 %copy-start.3 = (bf16[2,1152,128]{2,1,0:T(8,128)(2,1)S(1)}, bf16[2,1152,128]{2,1,0:T(8,128)(2,1)}, u32[]{:S(2)}) copy-start(bf16[2,1152,128]{2,1,0:T(8,128)(2,1)} %param.5) | copy-start | bytes 1769476
  6.5 1140.3 %all-reduce.3.cloned.1.call-start = ((), (), s32[]{:S(2)}) async-start(), calls=%async_computation | async-start | bytes 786432 | tf_op jit(solution)/shard_map/psum | solution.py:19
  145.0 0.7 copy-start.2
  1148.3 0.9 copy-start
  1148.3 1.0 copy-start.1
Sparse Core Ops, SparseCore 0:
  145.2 1001.5 all-reduce.2
where the time goes:
time: 1160 us
  waiting for transfers between devices  1000 us (86%)
  blocking collectives  133 us (11%)
  between operations  13.6 us (1%)
    psum x1, waiting for transfers between devices, scaled_coeffs(): summed = lax.psum(pair, 'space')  1000 us
    all_gather x3, blocking collectives, on_device(): whole_block = lax.all_gather(vectors[number], 'src', axis=2, tiled=True)  133 us
  transfers between devices with their start and end apart: 1, of which 1 were waited for; matrix products, arithmetic and copies ran while one was open for 0% of the time, Pallas kernels for 0%

commit v1 on v0

v1 whole, which is shorter than its diff:
```python
import jax
import jax.numpy as jnp
from jax import lax
from jax.experimental import pallas as pl
from jax.experimental.pallas import tpu as pltpu
from jax.sharding import PartitionSpec as P

G = 3
XS = 4
YS = 8
YL = 4
ZS = 16

YU, YD, PR, PI, L0, L1, R0, R1, O0, O1, QL0, QL1, QR0, QR1, QO0, QO1 = range(16)
EVENTS = 16


def kernel(
    vec, lam, srcs, out,
    vt, vrow, rhs1, rhs2, relay, acc,
    coef, crecv, zsrc, zrecv, ysrc, yrecv, sg,
    local_sem, ag_send, ag_recv,
    c_send, c_recv, z_send, z_recv, y_send, y_recv, s_send, s_recv, d_send, d_recv,
):
    me = lax.axis_index("src")
    space = lax.axis_index("space")
    x, h = me // 2, me % 2
    core, yl, z = space % 2, (space // 2) % YL, space // (2 * YL)
    y = h * YL + yl

    def at(x_, y_, z_, core_):
        return (x_ * 2 + y_ // YL, (z_ * YL + y_ % YL) * 2 + core_)

    right = at((x + 1) % XS, y, z, core)
    left = at((x + XS - 1) % XS, y, z, core)
    up = at(x, (y + 2) % YS, z, core)
    down = at(x, (y + YS - 2) % YS, z, core)
    sibling = at(x, y, z, 1 - core)
    z_peer = lambda k: at(x, y, (z + k) % ZS, core)
    y_peer = lambda k: at(x, h * YL + (yl + k) % YL, z, core)

    own = me
    mate = x * 2 + (1 - h)
    mate_up = x * 2 + (1 - ((y + 2) % YS) // YL)
    mate_down = x * 2 + (1 - ((y + YS - 2) % YS) // YL)
    xl, xr, xo = (x + XS - 1) % XS, (x + 1) % XS, (x + 2) % XS
    bl, br, bo = xl * 2 + h, xr * 2 + h, xo * 2 + h
    ql, qr, qo = xl * 2 + (1 - h), xr * 2 + (1 - h), xo * 2 + (1 - h)

    barrier = pltpu.get_barrier_semaphore()
    for peer in (right, left, up, down, sibling):
        pl.semaphore_signal(barrier, inc=1, device_id=peer, device_id_type=pl.DeviceIdType.MESH)
    for k in range(1, YL):
        pl.semaphore_signal(barrier, inc=1, device_id=y_peer(k), device_id_type=pl.DeviceIdType.MESH)

    @pl.loop(1, ZS)
    def _(k):
        pl.semaphore_signal(barrier, inc=1, device_id=z_peer(k), device_id_type=pl.DeviceIdType.MESH)

    loads = [
        pltpu.make_async_copy(vec, vt.at[:, :, own], local_sem.at[0]),
        pltpu.make_async_copy(srcs.at[0], rhs1.at[:, pl.ds(0, 128)], local_sem.at[1]),
        pltpu.make_async_copy(srcs.at[1], rhs1.at[:, pl.ds(128, 128)], local_sem.at[2]),
        pltpu.make_async_copy(srcs.at[1], rhs2.at[:, pl.ds(0, 128)], local_sem.at[3]),
    ]
    for load in loads:
        load.start()
    pl.semaphore_wait(barrier, 5 + (YL - 1) + (ZS - 1))

    sent = []

    def send(src, dst, g, event, device):
        copy = pltpu.make_async_remote_copy(
            src_ref=src, dst_ref=dst, send_sem=ag_send.at[g, event], recv_sem=ag_recv.at[g, event],
            device_id=device, device_id_type=pl.DeviceIdType.MESH,
        )
        copy.start()
        sent.append(copy)

    def arrived(region, g, event):
        pltpu.make_async_remote_copy(
            src_ref=region, dst_ref=region, send_sem=ag_send.at[g, event], recv_sem=ag_recv.at[g, event],
            device_id=right, device_id_type=pl.DeviceIdType.MESH,
        ).wait_recv()

    def start_own(g):
        send(vec.at[g, 0], relay.at[g, 0], g, YU, up)
        send(vec.at[g, 1], relay.at[g, 1], g, YD, down)
        send(vec.at[g, 0], vt.at[g, 0, own], g, L0, right)
        send(vec.at[g, 1], vt.at[g, 1, own], g, R1, left)
        send(vec.at[g, 1], vt.at[g, 1, own], g, L1, right)
        send(vec.at[g, 0], vt.at[g, 0, own], g, R0, left)

    def relay_y(g):
        arrived(relay.at[g, 0], g, YU)
        send(relay.at[g, 0], vt.at[g, 0, mate_up], g, PR, up)
        arrived(relay.at[g, 1], g, YD)
        send(relay.at[g, 1], vt.at[g, 1, mate_down], g, PI, down)

    def relay_x(g):
        arrived(vt.at[g, 0, bl], g, L0)
        send(vt.at[g, 0, bl], vt.at[g, 0, bl], g, O0, right)
        arrived(vt.at[g, 1, br], g, R1)
        send(vt.at[g, 1, br], vt.at[g, 1, br], g, O1, left)

    def start_mate(g):
        arrived(vt.at[g, 0, mate], g, PR)
        send(vt.at[g, 0, mate], vt.at[g, 0, mate], g, QL0, right)
        arrived(vt.at[g, 1, mate], g, PI)
        send(vt.at[g, 1, mate], vt.at[g, 1, mate], g, QR1, left)
        send(vt.at[g, 1, mate], vt.at[g, 1, mate], g, QL1, right)
        send(vt.at[g, 0, mate], vt.at[g, 0, mate], g, QR0, left)

    def relay_mate(g):
        arrived(vt.at[g, 0, ql], g, QL0)
        send(vt.at[g, 0, ql], vt.at[g, 0, ql], g, QO0, right)
        arrived(vt.at[g, 1, qr], g, QR1)
        send(vt.at[g, 1, qr], vt.at[g, 1, qr], g, QO1, left)

    def finish_gather(g):
        for event, c, block in (
            (L1, 1, bl), (R0, 0, br), (O0, 0, bo), (O1, 1, bo),
            (QL1, 1, ql), (QR0, 0, qr), (QO0, 0, qo), (QO1, 1, qo),
        ):
            arrived(vt.at[g, c, block], g, event)

    c_copies = [
        pltpu.make_async_remote_copy(
            src_ref=coef.at[g, 1 - core], dst_ref=crecv.at[g], send_sem=c_send.at[g], recv_sem=c_recv.at[g],
            device_id=sibling, device_id_type=pl.DeviceIdType.MESH,
        )
        for g in range(G)
    ]
    d_copies = [
        pltpu.make_async_remote_copy(
            src_ref=sg.at[g, core], dst_ref=sg.at[g, core], send_sem=d_send.at[g], recv_sem=d_recv.at[g],
            device_id=sibling, device_id_type=pl.DeviceIdType.MESH,
        )
        for g in range(G)
    ]

    def project(g):
        part = jnp.dot(vt[g, 0].reshape(128, -1), rhs1[...], preferred_element_type=jnp.float32)
        part = part + jnp.dot(vt[g, 1].reshape(128, -1), rhs2[...], preferred_element_type=jnp.float32)
        for half in range(2):
            for c in range(2):
                coef[g, half, c] = part[64 * half : 64 * half + 64, 128 * c : 128 * c + 128]
        c_copies[g].start()

    def z_copy(g, k):
        return pltpu.make_async_remote_copy(
            src_ref=zsrc.at[g, (z + k) % ZS], dst_ref=zrecv.at[g, ZS - 1 - k],
            send_sem=z_send.at[g], recv_sem=z_recv.at[g],
            device_id=z_peer(k), device_id_type=pl.DeviceIdType.MESH,
        )

    def scatter_z(g):
        c_copies[g].wait_recv()
        zsrc[g] = (coef[g, core] + crecv[g]).reshape(ZS, 8, 128)

        @pl.loop(1, ZS)
        def _(k):
            z_copy(g, k).start()

    def all_of(ref, send_sem, recv_sem):
        return pltpu.make_async_remote_copy(
            src_ref=ref, dst_ref=ref, send_sem=send_sem, recv_sem=recv_sem,
            device_id=right, device_id_type=pl.DeviceIdType.MESH,
        )

    def y_copy(g, k):
        return pltpu.make_async_remote_copy(
            src_ref=ysrc.at[g], dst_ref=yrecv.at[g, YL - 1 - k],
            send_sem=y_send.at[g], recv_sem=y_recv.at[g],
            device_id=y_peer(k), device_id_type=pl.DeviceIdType.MESH,
        )

    def exchange_y(g):
        all_of(zrecv.at[g], z_send.at[g], z_recv.at[g]).wait_recv()
        total = zsrc[g, z]
        for k in range(ZS - 1):
            total = total + zrecv[g, k]
        ysrc[g] = total
        for k in range(1, YL):
            y_copy(g, k).start()

    row = lax.broadcasted_iota(jnp.int32, (8, 128), 0)

    def s_copy(g, k):
        return pltpu.make_async_remote_copy(
            src_ref=sg.at[g, core, z], dst_ref=sg.at[g, core, z],
            send_sem=s_send.at[g], recv_sem=s_recv.at[g],
            device_id=z_peer(k), device_id_type=pl.DeviceIdType.MESH,
        )

    def scale(g):
        first = 64 * core + 8 * (z % 8)
        values = jnp.full((8, 128), lam[g, first], jnp.float32)
        for i in range(1, 8):
            values = jnp.where(row == i, lam[g, first + i], values)
        inverse = 1.0 / values
        all_of(yrecv.at[g], y_send.at[g], y_recv.at[g]).wait_recv()
        total = ysrc[g] + yrecv[g, 0] + yrecv[g, 1] + yrecv[g, 2]
        sg[g, core, z] = (total * inverse).astype(jnp.bfloat16).astype(jnp.float32)

        @pl.loop(1, ZS)
        def _(k):
            s_copy(g, k).start()

    def share(g):
        all_of(sg.at[g, core, pl.ds(0, ZS - 1)], s_send.at[g], s_recv.at[g]).wait_recv()
        d_copies[g].start()

    def transposed(g):
        for c in range(2):
            vrow[g, :, 128 * c : 128 * c + 128] = vt[g, c].reshape(128, -1).T

    def expand(g):
        all_of(sg.at[g, 1 - core], d_send.at[g], d_recv.at[g]).wait_recv()
        re = jnp.concatenate([sg[g, 0, 0:8].reshape(64, 128), sg[g, 1, 0:8].reshape(64, 128)], axis=0)
        im = jnp.concatenate([sg[g, 0, 8:16].reshape(64, 128), sg[g, 1, 8:16].reshape(64, 128)], axis=0)
        re = re.astype(jnp.bfloat16)
        im = im.astype(jnp.bfloat16)
        factor = jnp.concatenate(
            [jnp.concatenate([re, im], axis=1), jnp.concatenate([-im, re], axis=1)], axis=0
        )
        product = jnp.dot(vrow[g], factor, preferred_element_type=jnp.float32)
        if g == 0:
            acc[...] = product
        elif g < G - 1:
            acc[...] += product
        else:
            total = (acc[...] + product).astype(jnp.bfloat16)
            out[0] = total[:, :128]
            out[1] = total[:, 128:]

    for g in range(G):
        start_own(g)
    for load in loads:
        load.wait()
    rhs2[:, 128:256] = -rhs1[:, 0:128]

    relay_y(0)
    relay_x(0)
    relay_y(1)
    relay_x(1)
    start_mate(0)
    relay_y(2)
    relay_x(2)
    start_mate(1)
    relay_mate(0)
    start_mate(2)
    finish_gather(0)
    project(0)
    relay_mate(1)
    scatter_z(0)
    finish_gather(1)
    project(1)
    relay_mate(2)
    scatter_z(1)
    finish_gather(2)
    project(2)
    scatter_z(2)
    for g in range(G):
        transposed(g)
    exchange_y(0)
    exchange_y(1)
    scale(0)
    exchange_y(2)
    scale(1)
    scale(2)
    share(0)
    expand(0)
    share(1)
    expand(1)
    share(2)
    expand(2)

    for copy in sent:
        copy.wait_send()
    for g in range(G):
        c_copies[g].wait_send()
        d_copies[g].wait_send()
        all_of(zrecv.at[g], z_send.at[g], z_recv.at[g]).wait_send()
        all_of(yrecv.at[g], y_send.at[g], y_recv.at[g]).wait_send()
        all_of(sg.at[g, core, pl.ds(0, ZS - 1)], s_send.at[g], s_recv.at[g]).wait_send()


def on_device(vectors, lambdas, sources):
    rows = sources.shape[1]
    cols = sources.shape[2]
    vec = jnp.transpose(vectors, (0, 1, 3, 2))
    f32, bf16 = jnp.float32, jnp.bfloat16
    dma = pltpu.SemaphoreType.DMA
    return pl.pallas_call(
        kernel,
        out_shape=jax.ShapeDtypeStruct((2, rows, cols), bf16),
        in_specs=[
            pl.BlockSpec(memory_space=pl.ANY),
            pl.BlockSpec(memory_space=pltpu.SMEM),
            pl.BlockSpec(memory_space=pl.ANY),
        ],
        out_specs=pl.BlockSpec(memory_space=pltpu.VMEM),
        scratch_shapes=[
            pltpu.VMEM((G, 2, 8, 16, rows), bf16),
            pltpu.VMEM((G, rows, 256), bf16),
            pltpu.VMEM((rows, 256), bf16),
            pltpu.VMEM((rows, 256), bf16),
            pltpu.VMEM((G, 2, 16, rows), bf16),
            pltpu.VMEM((rows, 256), f32),
            pltpu.VMEM((G, 2, 2, 64, 128), f32),
            pltpu.VMEM((G, 2, 64, 128), f32),
            pltpu.VMEM((G, ZS, 8, 128), f32),
            pltpu.VMEM((G, ZS - 1, 8, 128), f32),
            pltpu.VMEM((G, 8, 128), f32),
            pltpu.VMEM((G, YL - 1, 8, 128), f32),
            pltpu.VMEM((G, 2, ZS, 8, 128), f32),
            dma((4,)),
            dma((G, EVENTS)),
            dma((G, EVENTS)),
            dma((G,)), dma((G,)), dma((G,)), dma((G,)), dma((G,)), dma((G,)),
            dma((G,)), dma((G,)), dma((G,)), dma((G,)),
        ],
        compiler_params=pltpu.CompilerParams(collective_id=0, has_side_effects=True),
    )(vec, lambdas, sources)


def solution(mesh):
    placed = (P(None, None, "space", "src"), P(), P(None, "space", "src"))
    return jax.shard_map(
        on_device, mesh=mesh, in_specs=placed, out_specs=P(None, "space", "src"), check_vma=False
    )
```

time: 1160 us -> 77.6 us (0.07)
  waiting for transfers between devices: 1000 us -> 0 us
  blocking collectives: 133 us -> 0 us
  Pallas kernels: 0 us -> 75.5 us
  between operations: 13.6 us -> 0.01 us
    psum x1 -> x0, waiting for transfers between devices: 1000 us -> none  [scaled_coeffs(): summed = lax.psum(pair, 'space')]
    all_gather x3 -> x0, blocking collectives: 133 us -> none  [on_device(): whole_block = lax.all_gather(vectors[number], 'src', axis=2, tiled=True)]
    pallas_call x0 -> x1, Pallas kernels: none -> 75.5 us  [on_device(): pl.pallas_call(kernel, out_shape=jax.ShapeDtypeStruct((2, rows, cols), bf...]
  transfers between devices with their start and end apart: 1 -> 0, of which waited for: 1 -> 0; matrix products, arithmetic and copies ran while one was open for 0% -> 0% of each run, Pallas kernels for 0% -> 0%
where the time goes in v1:
time: 77.6 us; the launch traced here: 77.4 us
  Pallas kernels  75.5 us (97%)
  local copies, waits for them, and re-layouts  1.92 us (2%)
    pallas_call x1, Pallas kernels, on_device(): pl.pallas_call(kernel, out_shape=jax.ShapeDtypeStruct((2, rows, cols), bf...  75.5 us
    unnamed x1, local copies, waits for them, and re-layouts  1.92 us

profile of v1, /device:TPU:1, one launch (start us, length us, event | category | flops | bytes accessed | tf_op | source)
XLA Modules:
  0.0 77.4 jit_solution(2837004387820505043)
XLA Ops:
  0.0 75.5 %shard_map.37 = bf16[2,1152,128]{2,1,0:T(8,128)(2,1)} custom-call(bf16[3,2,16,1152]{3,2,1,0:T(8,128)(2,1)} %bitcast.1, f32[3,128]{1,0:T(4,128)} %lam.1, bf16[2,1152,128]{2,1,0:T(8,128)(2,1)} %srcs.1), custom_call_target="tpu_custom_call" | custom-call | tf_op jit(solution)/shard_map/pallas_call | solution.py:295
  75.5 1.9 %copy.5 = bf16[2,1152,128]{2,1,0:T(8,128)(2,1)} copy(bf16[2,1152,128]{2,1,0:T(8,128)(2,1)} %shard_map.37) | data formatting | bytes 1179648

commit v2 on v1

--- a/solution.py
+++ b/solution.py
@@ -11,15 +11,15 @@
 YL = 4
 ZS = 16
 
-YU, YD, PR, PI, L0, L1, R0, R1, O0, O1, QL0, QL1, QR0, QR1, QO0, QO1 = range(16)
-EVENTS = 16
+PR, PI, L0, L1, R0, R1, O0, O1, QL0, QL1, QR0, QR1, QO0, QO1 = range(14)
+EVENTS = 14
 
 
 def kernel(
     vec, lam, srcs, out,
-    vt, vrow, rhs1, rhs2, relay, acc,
+    vt, vrow, rhs1, rhs2, acc,
     coef, crecv, zsrc, zrecv, ysrc, yrecv, sg,
-    local_sem, ag_send, ag_recv,
+    ready, local_sem, ag_send, ag_recv,
     c_send, c_recv, z_send, z_recv, y_send, y_recv, s_send, s_recv, d_send, d_recv,
 ):
     me = lax.axis_index("src")
@@ -33,29 +33,38 @@
 
     right = at((x + 1) % XS, y, z, core)
     left = at((x + XS - 1) % XS, y, z, core)
-    up = at(x, (y + 2) % YS, z, core)
-    down = at(x, (y + YS - 2) % YS, z, core)
+    across = at(x, (y + YL) % YS, z, core)
     sibling = at(x, y, z, 1 - core)
     z_peer = lambda k: at(x, y, (z + k) % ZS, core)
     y_peer = lambda k: at(x, h * YL + (yl + k) % YL, z, core)
 
     own = me
     mate = x * 2 + (1 - h)
-    mate_up = x * 2 + (1 - ((y + 2) % YS) // YL)
-    mate_down = x * 2 + (1 - ((y + YS - 2) % YS) // YL)
     xl, xr, xo = (x + XS - 1) % XS, (x + 1) % XS, (x + 2) % XS
     bl, br, bo = xl * 2 + h, xr * 2 + h, xo * 2 + h
     ql, qr, qo = xl * 2 + (1 - h), xr * 2 + (1 - h), xo * 2 + (1 - h)
 
+    def signal(semaphore, device):
+        pl.semaphore_signal(semaphore, inc=1, device_id=device, device_id_type=pl.DeviceIdType.MESH)
+
+    def greet(semaphore, step):
+        pl.when(z >= step)(lambda: signal(semaphore, at(x, y, z - step, core)))
+        pl.when(z + step < ZS)(lambda: signal(semaphore, at(x, y, z + step, core)))
+
+    def greeters(step):
+        return jnp.where(z >= step, 1, 0) + jnp.where(z + step < ZS, 1, 0)
+
     barrier = pltpu.get_barrier_semaphore()
-    for peer in (right, left, up, down, sibling):
-        pl.semaphore_signal(barrier, inc=1, device_id=peer, device_id_type=pl.DeviceIdType.MESH)
+    for peer in (right, left, across, sibling):
+        signal(barrier, peer)
     for k in range(1, YL):
-        pl.semaphore_signal(barrier, inc=1, device_id=y_peer(k), device_id_type=pl.DeviceIdType.MESH)
-
-    @pl.loop(1, ZS)
-    def _(k):
-        pl.semaphore_signal(barrier, inc=1, device_id=z_peer(k), device_id_type=pl.DeviceIdType.MESH)
+        signal(barrier, y_peer(k))
+    greet(barrier, 1)
+
+    def meet(round_):
+        pl.semaphore_wait(ready.at[round_], greeters(1 << round_))
+        if round_ < 3:
+            greet(ready.at[round_ + 1], 2 << round_)
 
     loads = [
         pltpu.make_async_copy(vec, vt.at[:, :, own], local_sem.at[0]),
@@ -65,7 +74,8 @@
     ]
     for load in loads:
         load.start()
-    pl.semaphore_wait(barrier, 5 + (YL - 1) + (ZS - 1))
+    pl.semaphore_wait(barrier, 4 + (YL - 1) + greeters(1))
+    greet(ready.at[0], 1)
 
     sent = []
 
@@ -84,18 +94,12 @@
         ).wait_recv()
 
     def start_own(g):
-        send(vec.at[g, 0], relay.at[g, 0], g, YU, up)
-        send(vec.at[g, 1], relay.at[g, 1], g, YD, down)
+        send(vec.at[g, 0], vt.at[g, 0, own], g, PR, across)
+        send(vec.at[g, 1], vt.at[g, 1, own], g, PI, across)
         send(vec.at[g, 0], vt.at[g, 0, own], g, L0, right)
         send(vec.at[g, 1], vt.at[g, 1, own], g, R1, left)
         send(vec.at[g, 1], vt.at[g, 1, own], g, L1, right)
         send(vec.at[g, 0], vt.at[g, 0, own], g, R0, left)
-
-    def relay_y(g):
-        arrived(relay.at[g, 0], g, YU)
-        send(relay.at[g, 0], vt.at[g, 0, mate_up], g, PR, up)
-        arrived(relay.at[g, 1], g, YD)
-        send(relay.at[g, 1], vt.at[g, 1, mate_down], g, PI, down)
 
     def relay_x(g):
         arrived(vt.at[g, 0, bl], g, L0)
@@ -147,6 +151,9 @@
                 coef[g, half, c] = part[64 * half : 64 * half + 64, 128 * c : 128 * c + 128]
         c_copies[g].start()
 
+    def far_first(j):
+        return ZS // 2 + ((j + 1) // 2) * (2 * ((j + 1) % 2) - 1)
+
     def z_copy(g, k):
         return pltpu.make_async_remote_copy(
             src_ref=zsrc.at[g, (z + k) % ZS], dst_ref=zrecv.at[g, ZS - 1 - k],
@@ -158,9 +165,9 @@
         c_copies[g].wait_recv()
         zsrc[g] = (coef[g, core] + crecv[g]).reshape(ZS, 8, 128)
 
-        @pl.loop(1, ZS)
-        def _(k):
-            z_copy(g, k).start()
+        @pl.loop(0, ZS - 1)
+        def _(j):
+            z_copy(g, far_first(j)).start()
 
     def all_of(ref, send_sem, recv_sem):
         return pltpu.make_async_remote_copy(
@@ -201,11 +208,11 @@
         inverse = 1.0 / values
         all_of(yrecv.at[g], y_send.at[g], y_recv.at[g]).wait_recv()
         total = ysrc[g] + yrecv[g, 0] + yrecv[g, 1] + yrecv[g, 2]
-        sg[g, core, z] = (total * inverse).astype(jnp.bfloat16).astype(jnp.float32)
-
-        @pl.loop(1, ZS)
-        def _(k):
-            s_copy(g, k).start()
+        sg[g, core, z] = (total * inverse).astype(jnp.bfloat16)
+
+        @pl.loop(0, ZS - 1)
+        def _(j):
+            s_copy(g, far_first(j)).start()
 
     def share(g):
         all_of(sg.at[g, core, pl.ds(0, ZS - 1)], s_send.at[g], s_recv.at[g]).wait_recv()
@@ -217,10 +224,11 @@
 
     def expand(g):
         all_of(sg.at[g, 1 - core], d_send.at[g], d_recv.at[g]).wait_recv()
-        re = jnp.concatenate([sg[g, 0, 0:8].reshape(64, 128), sg[g, 1, 0:8].reshape(64, 128)], axis=0)
-        im = jnp.concatenate([sg[g, 0, 8:16].reshape(64, 128), sg[g, 1, 8:16].reshape(64, 128)], axis=0)
-        re = re.astype(jnp.bfloat16)
-        im = im.astype(jnp.bfloat16)
+        tiles = lambda part: [
+            sg[g, half, part].astype(jnp.float32).reshape(64, 128) for half in range(2)
+        ]
+        re = jnp.concatenate(tiles(slice(0, 8)), axis=0).astype(jnp.bfloat16)
+        im = jnp.concatenate(tiles(slice(8, 16)), axis=0).astype(jnp.bfloat16)
         factor = jnp.concatenate(
             [jnp.concatenate([re, im], axis=1), jnp.concatenate([-im, re], axis=1)], axis=0
         )
@@ -230,7 +238,7 @@
         elif g < G - 1:
             acc[...] += product
         else:
-            total = (acc[...] + product).astype(jnp.bfloat16)
+            total = acc[...] + product
             out[0] = total[:, :128]
             out[1] = total[:, 128:]
 
@@ -240,23 +248,24 @@
         load.wait()
     rhs2[:, 128:256] = -rhs1[:, 0:128]
 
-    relay_y(0)
+    meet(0)
     relay_x(0)
-    relay_y(1)
     relay_x(1)
+    meet(1)
+    relay_x(2)
     start_mate(0)
-    relay_y(2)
-    relay_x(2)
+    meet(2)
     start_mate(1)
     relay_mate(0)
     start_mate(2)
+    relay_mate(1)
     finish_gather(0)
     project(0)
-    relay_mate(1)
+    meet(3)
     scatter_z(0)
+    relay_mate(2)
     finish_gather(1)
     project(1)
-    relay_mate(2)
     scatter_z(1)
     finish_gather(2)
     project(2)
@@ -292,9 +301,9 @@
     vec = jnp.transpose(vectors, (0, 1, 3, 2))
     f32, bf16 = jnp.float32, jnp.bfloat16
     dma = pltpu.SemaphoreType.DMA
-    return pl.pallas_call(
+    total = pl.pallas_call(
         kernel,
-        out_shape=jax.ShapeDtypeStruct((2, rows, cols), bf16),
+        out_shape=jax.ShapeDtypeStruct((2, rows, cols), f32),
         in_specs=[
             pl.BlockSpec(memory_space=pl.ANY),
             pl.BlockSpec(memory_space=pltpu.SMEM),
@@ -306,7 +315,6 @@
             pltpu.VMEM((G, rows, 256), bf16),
             pltpu.VMEM((rows, 256), bf16),
             pltpu.VMEM((rows, 256), bf16),
-            pltpu.VMEM((G, 2, 16, rows), bf16),
             pltpu.VMEM((rows, 256), f32),
             pltpu.VMEM((G, 2, 2, 64, 128), f32),
             pltpu.VMEM((G, 2, 64, 128), f32),
@@ -314,7 +322,8 @@
             pltpu.VMEM((G, ZS - 1, 8, 128), f32),
             pltpu.VMEM((G, 8, 128), f32),
             pltpu.VMEM((G, YL - 1, 8, 128), f32),
-            pltpu.VMEM((G, 2, ZS, 8, 128), f32),
+            pltpu.VMEM((G, 2, ZS, 8, 128), bf16),
+            pltpu.SemaphoreType.REGULAR((4,)),
             dma((4,)),
             dma((G, EVENTS)),
             dma((G, EVENTS)),
@@ -323,6 +332,7 @@
         ],
         compiler_params=pltpu.CompilerParams(collective_id=0, has_side_effects=True),
     )(vec, lambdas, sources)
+    return total.astype(bf16)
 
 
 def solution(mesh):

time: 77.6 us -> 68 us (0.88)
  Pallas kernels: 75.5 us -> 65.6 us
  other arithmetic: 0 us -> 2.16 us
  local copies, waits for them, and re-layouts: 1.92 us -> 0 us
    pallas_call x1, Pallas kernels: 75.5 us -> 65.6 us  [on_device(): pl.pallas_call(kernel, out_shape=jax.ShapeDtypeStruct((2, rows, cols), f3...]
    convert_element_type x0 -> x1, other arithmetic: none -> 2.16 us  [on_device(): return total.astype(bf16)]
    unnamed x1 -> x0, local copies, waits for them, and re-layouts: 1.92 us -> none
where the time goes in v2:
time: 68 us; the launch traced here: 67.8 us
  Pallas kernels  65.6 us (96%)
  other arithmetic  2.16 us (3%)
    pallas_call x1, Pallas kernels, on_device(): pl.pallas_call(kernel, out_shape=jax.ShapeDtypeStruct((2, rows, cols), f3...  65.6 us
    convert_element_type x1, other arithmetic, on_device(): return total.astype(bf16)  2.16 us

profile of v2, /device:TPU:1, one launch (start us, length us, event | category | flops | bytes accessed | tf_op | source)
XLA Modules:
  0.0 67.8 jit_solution(17942390610649701478)
XLA Ops:
  0.0 65.6 %shard_map.37 = f32[2,1152,128]{2,1,0:T(8,128)} custom-call(bf16[3,2,16,1152]{3,2,1,0:T(8,128)(2,1)} %bitcast.1, f32[3,128]{1,0:T(4,128)} %lam.1, bf16[2,1152,128]{2,1,0:T(8,128)(2,1)} %srcs.1), custom_call_target="tpu_custom_call" | custom-call | tf_op jit(solution)/shard_map/pallas_call | solution.py:304
  65.6 2.2 %convert_element_type.3 = bf16[2,1152,128]{2,1,0:T(8,128)(2,1)} convert(f32[2,1152,128]{2,1,0:T(8,128)} %shard_map.37) | non-fusion elementwise | flops 294912 | bytes 1769472 | tf_op jit(solution)/shard_map/convert_element_type | solution.py:335

commit v3 on v2

--- a/solution.py
+++ b/solution.py
@@ -121,11 +121,18 @@
         arrived(vt.at[g, 1, qr], g, QR1)
         send(vt.at[g, 1, qr], vt.at[g, 1, qr], g, QO1, left)
 
+    def opposite_across(g):
+        for event, c, mate_event in ((O0, 0, QO0), (O1, 1, QO1)):
+            arrived(vt.at[g, c, bo], g, event)
+            send(vt.at[g, c, bo], vt.at[g, c, bo], g, mate_event, across)
+
     def finish_gather(g):
         for event, c, block in (
-            (L1, 1, bl), (R0, 0, br), (O0, 0, bo), (O1, 1, bo),
+            (L1, 1, bl), (R0, 0, br), (O0, 0, bo), (O1, 1, bo), (QL0, 0, ql), (QR1, 1, qr),
             (QL1, 1, ql), (QR0, 0, qr), (QO0, 0, qo), (QO1, 1, qo),
         ):
+            if event in ((QL0, QR1) if g < G - 1 else (O0, O1)):
+                continue
             arrived(vt.at[g, c, block], g, event)
 
     c_copies = [
@@ -135,14 +142,6 @@
         )
         for g in range(G)
     ]
-    d_copies = [
-        pltpu.make_async_remote_copy(
-            src_ref=sg.at[g, core], dst_ref=sg.at[g, core], send_sem=d_send.at[g], recv_sem=d_recv.at[g],
-            device_id=sibling, device_id_type=pl.DeviceIdType.MESH,
-        )
-        for g in range(G)
-    ]
-
     def project(g):
         part = jnp.dot(vt[g, 0].reshape(128, -1), rhs1[...], preferred_element_type=jnp.float32)
         part = part + jnp.dot(vt[g, 1].reshape(128, -1), rhs2[...], preferred_element_type=jnp.float32)
@@ -165,8 +164,7 @@
         c_copies[g].wait_recv()
         zsrc[g] = (coef[g, core] + crecv[g]).reshape(ZS, 8, 128)
 
-        @pl.loop(0, ZS - 1)
-        def _(j):
+        for j in range(ZS - 1):
             z_copy(g, far_first(j)).start()
 
     def all_of(ref, send_sem, recv_sem):
@@ -197,7 +195,14 @@
         return pltpu.make_async_remote_copy(
             src_ref=sg.at[g, core, z], dst_ref=sg.at[g, core, z],
             send_sem=s_send.at[g], recv_sem=s_recv.at[g],
-            device_id=z_peer(k), device_id_type=pl.DeviceIdType.MESH,
+            device_id=at(x, y, k, core), device_id_type=pl.DeviceIdType.MESH,
+        )
+
+    def d_copy(g, k):
+        return pltpu.make_async_remote_copy(
+            src_ref=sg.at[g, core, z], dst_ref=sg.at[g, core, z],
+            send_sem=d_send.at[g], recv_sem=d_recv.at[g],
+            device_id=at(x, y, k, 1 - core), device_id_type=pl.DeviceIdType.MESH,
         )
 
     def scale(g):
@@ -210,13 +215,15 @@
         total = ysrc[g] + yrecv[g, 0] + yrecv[g, 1] + yrecv[g, 2]
         sg[g, core, z] = (total * inverse).astype(jnp.bfloat16)
 
-        @pl.loop(0, ZS - 1)
-        def _(j):
-            s_copy(g, far_first(j)).start()
+        for target in range(ZS):
+            d_copy(g, target).start()
+
+            @pl.when(z != target)
+            def _(target=target):
+                s_copy(g, target).start()
 
     def share(g):
         all_of(sg.at[g, core, pl.ds(0, ZS - 1)], s_send.at[g], s_recv.at[g]).wait_recv()
-        d_copies[g].start()
 
     def transposed(g):
         for c in range(2):
@@ -255,15 +262,15 @@
     relay_x(2)
     start_mate(0)
     meet(2)
+    opposite_across(2)
     start_mate(1)
     relay_mate(0)
-    start_mate(2)
     relay_mate(1)
     finish_gather(0)
     project(0)
+    start_mate(2)
     meet(3)
     scatter_z(0)
-    relay_mate(2)
     finish_gather(1)
     project(1)
     scatter_z(1)
@@ -289,7 +296,7 @@
         copy.wait_send()
     for g in range(G):
         c_copies[g].wait_send()
-        d_copies[g].wait_send()
+        all_of(sg.at[g, core], d_send.at[g], d_recv.at[g]).wait_send()
         all_of(zrecv.at[g], z_send.at[g], z_recv.at[g]).wait_send()
         all_of(yrecv.at[g], y_send.at[g], y_recv.at[g]).wait_send()
         all_of(sg.at[g, core, pl.ds(0, ZS - 1)], s_send.at[g], s_recv.at[g]).wait_send()

time: 68 us -> 66.5 us (0.978)
  Pallas kernels: 65.6 us -> 64.1 us
    pallas_call x1, Pallas kernels: 65.6 us -> 64.1 us  [on_device(): pl.pallas_call(kernel, out_shape=jax.ShapeDtypeStruct((2, rows, cols), f3...]
where the time goes in v3:
time: 66.5 us; the launch traced here: 66.2 us
  Pallas kernels  64.1 us (96%)
  other arithmetic  2.16 us (3%)
    pallas_call x1, Pallas kernels, on_device(): pl.pallas_call(kernel, out_shape=jax.ShapeDtypeStruct((2, rows, cols), f3...  64.1 us
    convert_element_type x1, other arithmetic, on_device(): return total.astype(bf16)  2.16 us

profile of v3, /device:TPU:1, one launch (start us, length us, event | category | flops | bytes accessed | tf_op | source)
XLA Modules:
  0.0 66.2 jit_solution(2095380286300396755)
XLA Ops:
  0.0 64.1 %shard_map.37 = f32[2,1152,128]{2,1,0:T(8,128)} custom-call(bf16[3,2,16,1152]{3,2,1,0:T(8,128)(2,1)} %bitcast.1, f32[3,128]{1,0:T(4,128)} %lam.1, bf16[2,1152,128]{2,1,0:T(8,128)(2,1)} %srcs.1), custom_call_target="tpu_custom_call" | custom-call | tf_op jit(solution)/shard_map/pallas_call | solution.py:311
  64.1 2.2 %convert_element_type.3 = bf16[2,1152,128]{2,1,0:T(8,128)(2,1)} convert(f32[2,1152,128]{2,1,0:T(8,128)} %shard_map.37) | non-fusion elementwise | flops 294912 | bytes 1769472 | tf_op jit(solution)/shard_map/convert_element_type | solution.py:342

commit v4 on v3

--- a/solution.py
+++ b/solution.py
@@ -10,6 +10,7 @@
 YS = 8
 YL = 4
 ZS = 16
+DIRECT = (2,)
 
 PR, PI, L0, L1, R0, R1, O0, O1, QL0, QL1, QR0, QR1, QO0, QO1 = range(14)
 EVENTS = 14
@@ -216,7 +217,8 @@
         sg[g, core, z] = (total * inverse).astype(jnp.bfloat16)
 
         for target in range(ZS):
-            d_copy(g, target).start()
+            if g in DIRECT:
+                d_copy(g, target).start()
 
             @pl.when(z != target)
             def _(target=target):
@@ -224,6 +226,11 @@
 
     def share(g):
         all_of(sg.at[g, core, pl.ds(0, ZS - 1)], s_send.at[g], s_recv.at[g]).wait_recv()
+        if g not in DIRECT:
+            pltpu.make_async_remote_copy(
+                src_ref=sg.at[g, core], dst_ref=sg.at[g, core], send_sem=d_send.at[g], recv_sem=d_recv.at[g],
+                device_id=sibling, device_id_type=pl.DeviceIdType.MESH,
+            ).start()
 
     def transposed(g):
         for c in range(2):
@@ -245,7 +252,7 @@
         elif g < G - 1:
             acc[...] += product
         else:
-            total = acc[...] + product
+            total = (acc[...] + product).astype(out.dtype)
             out[0] = total[:, :128]
             out[1] = total[:, 128:]
 
@@ -310,7 +317,7 @@
     dma = pltpu.SemaphoreType.DMA
     total = pl.pallas_call(
         kernel,
-        out_shape=jax.ShapeDtypeStruct((2, rows, cols), f32),
+        out_shape=pltpu.VMEM((2, rows, cols), bf16),
         in_specs=[
             pl.BlockSpec(memory_space=pl.ANY),
             pl.BlockSpec(memory_space=pltpu.SMEM),
@@ -339,7 +346,7 @@
         ],
         compiler_params=pltpu.CompilerParams(collective_id=0, has_side_effects=True),
     )(vec, lambdas, sources)
-    return total.astype(bf16)
+    return total
 
 
 def solution(mesh):

time: 66.5 us -> 63.7 us (0.958)
  other arithmetic: 2.16 us -> 0 us
  Pallas kernels: 64.1 us -> 62.7 us
  local copies, waits for them, and re-layouts: 0 us -> 0.82 us
    convert_element_type x1 -> x0, other arithmetic: 2.16 us -> none  [on_device(): return total.astype(bf16)]
    pallas_call x1, Pallas kernels: 64.1 us -> 62.7 us  [on_device(): pl.pallas_call(kernel, out_shape=pltpu.VMEM((2, rows, cols), bf16), in_sp...]
    unnamed x0 -> x1, local copies, waits for them, and re-layouts: none -> 0.82 us
where the time goes in v4:
time: 63.7 us; the launch traced here: 63.5 us
  Pallas kernels  62.7 us (98%)
  local copies, waits for them, and re-layouts  0.82 us (1%)
    pallas_call x1, Pallas kernels, on_device(): pl.pallas_call(kernel, out_shape=pltpu.VMEM((2, rows, cols), bf16), in_sp...  62.7 us

profile of v4, /device:TPU:1, one launch (start us, length us, event | category | flops | bytes accessed | tf_op | source)
XLA Modules:
  0.0 63.5 jit_solution(17552625316748577313)
XLA Ops:
  0.0 62.7 %shard_map.37 = bf16[2,1152,128]{2,1,0:T(8,128)(2,1)S(1)} custom-call(bf16[3,2,16,1152]{3,2,1,0:T(8,128)(2,1)} %bitcast.1, f32[3,128]{1,0:T(4,128)} %lam.1, bf16[2,1152,128]{2,1,0:T(8,128)(2,1)} %srcs.1), custom_call_target="tpu_custom_call" | custom-call | tf_op jit(solution)/shard_map/pallas_call | solution.py:318
  62.7 0.8 %copy.5 = bf16[2,1152,128]{2,1,0:T(8,128)(2,1)} copy(bf16[2,1152,128]{2,1,0:T(8,128)(2,1)S(1)} %shard_map.37) | data formatting | bytes 1179648
